TPU v7x, 32 devices: a whole 2x2x4 slice. The times are simulated.
32 devices in a mesh: sep: 4 (over x, core), sub: 8 (over z, y).
Axes of the slice: x: 2, y: 2, z: 4, core: 2. Of those that a mesh axis runs over, the one named last changes fastest.
Arguments:
- g_top: bfloat16 [2048, 2048], P('sub', 'sep'), may hold values from -8 to 32, as said below
- u_mid: bfloat16 [4, 2048, 512], P('sep', 'sub'), may hold values from -0.125 to 0.125
- b_mid: float32 [4, 512, 512], P('sep', 'sub'), may hold values from -8 to 32
- u_leaf: bfloat16 [32, 1536, 1536], P(('sep', 'sub')), may hold values from -0.15625 to 0.15625
- leaf_index: int32 [32, 1536], P(('sep', 'sub')), may hold values from 0 to 2559, as said below
- leaf_count: int32 [32], P(('sep', 'sub')), may hold values from 768 to 1536, as said below
- leaf_bdiag: float32 [32, 1536], P(('sep', 'sub')), may hold values from 4 to 16
Outputs:
- mid_cross: bfloat16 [4, 2048, 512], P('sep', 'sub')
- mid_block: bfloat16 [4, 512, 512], P('sep', 'sub')
- leaf_offdiag: bfloat16 [32, 1536, 1536], P(('sep', 'sub'))
- leaf_diag: float32 [32, 1536], P(('sep', 'sub'))
Inputs may be any that keep to these rules, and one draw needn't show every extreme that they name: g_top is symmetric. `leaf_index`: A leaf's 1536 entries are distinct; an entry below 2048 is a row of the top separator, an entry r of 2048 or more is row r - 2048 of the leaf's middle separator. `leaf_count`: some leaf has all 1536 slots live.
All inputs are finite; a program needn't handle non-finite values.
Results may differ from a plain program's by a relative error of at most 0.004.
Values may be sent and summed in bfloat16 or wider, within the bound.
A program may use at most 128 MiB of HBM per device.

v0:
```python
import jax
import jax.numpy as jnp
from jax import lax
from jax.sharding import PartitionSpec as P

NT = 2048


def shards(g_top, u_mid, b_mid, u_leaf, leaf_index, leaf_count, leaf_bdiag):
    top_rows = lax.all_gather(g_top, "sep", axis=1, tiled=True)
    factor = u_mid[0]
    summed = jnp.dot(
        top_rows,
        lax.all_gather(factor, "sub", axis=0, tiled=True),
        preferred_element_type=jnp.float32,
    )
    cross_rows = (-summed).astype(jnp.bfloat16)
    own_block = b_mid[0]
    mid_rows = (
        own_block
        - lax.psum_scatter(
            lax.dot_general(
                factor, cross_rows, (((0,), (0,)), ((), ())), preferred_element_type=jnp.float32
            ),
            "sub",
            scatter_dimension=0,
            tiled=True,
        )
    ).astype(jnp.bfloat16)
    slot_index = leaf_index[0]
    slots = slot_index.shape[0]
    top_side = slot_index < NT
    clipped = jnp.minimum(slot_index, NT - 1)
    midpos = jnp.maximum(slot_index - NT, 0)
    upper_own = jnp.concatenate([top_rows, cross_rows], axis=1)
    upper_rows, whole_block = (
        lax.all_gather(upper_own, "sub", axis=0, tiled=True),
        lax.all_gather(mid_rows, "sub", axis=0, tiled=True),
    )
    picked = jnp.take(jnp.take(upper_rows, clipped, axis=0), slot_index, axis=1)
    mid_mid = jnp.take(jnp.take(whole_block, midpos, axis=0), midpos, axis=1)
    chosen = jnp.where(top_side[:, None], picked, jnp.where(top_side[None, :], picked.T, mid_mid))
    live_slot = jnp.arange(slots, dtype=jnp.int32) < leaf_count[0]
    masked = jnp.where(live_slot[:, None], u_leaf[0], jnp.zeros((), u_leaf.dtype))
    product = jnp.dot(chosen, masked, preferred_element_type=jnp.float32)
    offdiag = jnp.where(live_slot[:, None], -product, jnp.zeros((), jnp.float32)).astype(
        jnp.bfloat16
    )
    diagonal = leaf_bdiag[0] + jnp.sum(masked.astype(jnp.float32) * product, axis=0)
    return (cross_rows[None], mid_rows[None], offdiag[None], diagonal[None])


def solution(mesh):
    return jax.shard_map(
        shards,
        mesh=mesh,
        in_specs=(
            P("sub", "sep"),
            P("sep", "sub", None),
            P("sep", "sub", None),
            P(("sep", "sub"), None, None),
            P(("sep", "sub"), None),
            P(("sep", "sub")),
            P(("sep", "sub"), None),
        ),
        out_specs=(
            P("sep", "sub", None),
            P("sep", "sub", None),
            P(("sep", "sub"), None, None),
            P(("sep", "sub"), None),
        ),
        check_vma=False,
    )
```

profile of v0, /device:TPU:0, one launch (start us, length us, event | category | flops | bytes accessed | tf_op | source)
XLA Modules:
  0.0 393.3 jit_solution(875404517294818753)
XLA Ops:
  7.9 0.7 all-gather.9.cloned.1.call-update
  8.7 20.3 %all-gather.5.cloned.1.call-done = bf16[256,2048]{1,0:T(8,128)(2,1)} async-done(((bf16[256,512]{1,0:T(8,128)(2,1)}), bf16[256,2048]{1,0:T(8,128)(2,1)}) %all-gather.5.cloned.1.call-update) | async-done | bytes 1048592 | tf_op jit(solution)/shard_map/all_gather | solution.py:10
  29.0 51.3 %all-gather.9.cloned.1.call-done = bf16[1,2048,512]{2,1,0:T(8,128)(2,1)} async-done(((bf16[1,256,512]{2,1,0:T(8,128)(2,1)}), bf16[1,2048,512]{2,1,0:T(8,128)(2,1)}) %all-gather.9.cloned.1.call-update) | async-done | bytes 2097168 | tf_op jit(solution)/shard_map/all_gather | solution.py:14
  80.3 2.6 fusion.15
  82.9 1.4 convolution_bitcast_fusion
  84.3 1.3 copy.35
  85.7 1.2 pad_maximum_fusion
  87.9 60.5 %reduce-scatter.4.cloned.1.call-done = f32[64,512]{1,0:T(8,128)} async-done(((f32[512,512]{1,0:T(8,128)}), f32[64,512]{1,0:T(8,128)}) %reduce-scatter.4.cloned.1.call-update) | async-done | bytes 131088
  148.5 1.0 copy.36
  149.6 0.7 copy.34
  150.4 33.3 %all_gather.15 = bf16[512,512]{1,0:T(8,128)(2,1)S(1)} all-gather(bf16[64,512]{1,0:T(8,128)(2,1)S(1)} %copy.31), channel_id=1, replica_groups=mesh['sep'=4,'sub'=8] {'sub'}, dimensions={0}, use_global_device_ids=true | all-gather | bytes 589824 | tf_op jit(solution)/shard_map/all_gather | solution.py:38
  183.6 4.8 %gather_fusion.2 = bf16[1536,512]{1,0:T(8,128)(2,1)S(1)} fusion(bf16[512,512]{1,0:T(8,128)(2,1)S(1)} %all_gather.15, s32[2048]{0:T(1024)S(1)} %pad_clamp_fusion), kind=kCustom, calls=%fused_computation.2 | custom fusion | bytes 3151872 | tf_op jit(solution)/shard_map/jit(_take)/gather | solution.py:41
  188.5 1.4 broadcast_select_fusion.2
  189.9 1.7 copy.32
  191.6 6.2 %gather_fusion.3 = bf16[1536,1536]{1,0:T(8,128)(2,1)} fusion(bf16[1536,512]{0,1:T(8,128)(2,1)S(1)} %copy.32, s32[2048]{0:T(1024)S(1)} %pad_clamp_fusion), kind=kCustom, calls=%fused_computation.3 | custom fusion | bytes 9443328 | tf_op jit(solution)/shard_map/jit(_take)/gather | solution.py:41
  197.8 6.7 %copy.33 = bf16[1536,1536]{0,1:T(8,128)(2,1)} copy(bf16[1536,1536]{1,0:T(8,128)(2,1)} %gather_fusion.3) | data formatting | bytes 9437184 | tf_op jit(solution)/shard_map/jit(_take)/gather | solution.py:41
  204.4 98.6 %all-gather.7.cloned.1.call-done = bf16[2048,2560]{1,0:T(8,128)(2,1)} async-done(((bf16[256,2560]{1,0:T(8,128)(2,1)}), bf16[2048,2560]{1,0:T(8,128)(2,1)}) %all-gather.7.cloned.1.call-update) | async-done | bytes 10485776 | tf_op jit(solution)/shard_map/all_gather | solution.py:37
  303.0 20.4 %gather_fusion = bf16[1536,2560]{1,0:T(8,128)(2,1)} fusion(bf16[2048,2560]{1,0:T(8,128)(2,1)} %all-gather.7.cloned.1.call-done, s32[2048]{0:T(1024)S(1)} %pad_clamp_fusion.2), kind=kCustom, calls=%fused_computation | custom fusion | bytes 15734784 | tf_op jit(solution)/shard_map/jit(_take)/gather | solution.py:40
  323.5 7.2 %broadcast_select_fusion = bf16[1536,2560]{1,0:T(8,128)(2,1)} fusion(bf16[1536,2560]{1,0:T(8,128)(2,1)} %gather_fusion, pred[1536]{0:T(1024)(128)(4,1)S(1)} %get-tuple-element.23), kind=kLoop, calls=%fused_computation.6 | loop fusion | flops 3932160 | bytes 15730176 | tf_op jit(solution)/shard_map/jit(_take)/select_n | solution.py:40
  330.6 10.6 %copy.28 = bf16[1536,2560]{0,1:T(8,128)(2,1)} copy(bf16[1536,2560]{1,0:T(8,128)(2,1)} %broadcast_select_fusion) | data formatting | bytes 15728640 | tf_op jit(solution)/shard_map/jit(_take)/select_n | solution.py:40
  341.2 14.6 %gather_fusion.1 = bf16[1536,1536]{1,0:T(8,128)(2,1)} fusion(bf16[1536,2560]{0,1:T(8,128)(2,1)} %copy.28, s32[2048]{0:T(1024)S(1)} %pad_clamp_fusion.1), kind=kCustom, calls=%fused_computation.1 | custom fusion | bytes 9443328 | tf_op jit(solution)/shard_map/jit(_take)/gather | solution.py:40
  355.9 5.0 %broadcast_select_fusion.1 = bf16[1536,1536]{1,0:T(8,128)(2,1)} fusion(bf16[1536,1536]{1,0:T(8,128)(2,1)} %gather_fusion.1, pred[1536]{0:T(1024)(128)(4,1)S(1)} %get-tuple-element.22), kind=kLoop, calls=%fused_computation.14 | loop fusion | flops 2359296 | bytes 9438720 | tf_op jit(solution)/shard_map/jit(_take)/select_n | solution.py:40
  360.8 6.7 %copy.30 = bf16[1536,1536]{0,1:T(8,128)(2,1)} copy(bf16[1536,1536]{1,0:T(8,128)(2,1)} %broadcast_select_fusion.1) | data formatting | bytes 9437184 | tf_op jit(solution)/shard_map/jit(_take)/select_n | solution.py:40
  367.5 18.6 %multiply_reduce_fusion = (f32[1536]{0:T(1024)S(1)}, bf16[1,1536,1536]{2,1,0:T(8,128)(2,1)}) fusion(bf16[1,1536,1536]{2,1,0:T(8,128)(2,1)} %param.10, pred[1536]{0:T(1024)(128)(4,1)S(1)} %iota_compare_fusion, bf16[1536,1536]{1,0:T(8,128)(2,1)} %broadcast_select_fusion.1, bf16[1536,1536]{0,1:T(8,128)(2,1)} %copy.30, bf16[1536,1536]{0,1:T(8,128)(2,1)} %copy.33, ...), kind=kOutput, calls=%fused_computation.4 | convolution fusion | flops 7273708032 | bytes 23605248 | tf_op jit(solution)/shard_map/dot_general | solution.py:45
  (29 shorter events, 1.9 us)
Async XLA Ops:
  7.2 21.8 %all-gather.5.cloned.1.call-start = ((), (), s32[]{:S(2)}) async-start(), calls=%async_computation.1 | async-start | bytes 1310720 | tf_op jit(solution)/shard_map/all_gather | solution.py:10
  7.9 72.4 %all-gather.9.cloned.1.call-start = ((), (), s32[]{:S(2)}) async-start(), calls=%async_computation.3 | async-start | bytes 2359296 | tf_op jit(solution)/shard_map/all_gather | solution.py:14
  8.6 139.8 %reduce-scatter.4.cloned.1.call-start = ((), (), s32[]{:S(2)}) async-start(), calls=%async_computation.4 | async-start | bytes 1179648
  29.0 56.7 %copy-start = (bf16[256,2048]{1,0:T(8,128)(2,1)S(1)}, bf16[256,2048]{1,0:T(8,128)(2,1)}, u32[]{:S(2)}) copy-start(bf16[256,2048]{1,0:T(8,128)(2,1)} %all-gather.5.cloned.1.call-done) | copy-start | bytes 3145732
  82.9 66.6 %copy-start.1 = (bf16[256,512]{1,0:T(8,128)(2,1)}, bf16[256,512]{1,0:T(8,128)(2,1)S(1)}, u32[]{:S(2)}) copy-start(bf16[256,512]{1,0:T(8,128)(2,1)S(1)} %fusion.15) | copy-start | bytes 786436
  82.9 4.7 %copy-start.2 = (f32[1,64,512]{2,1,0:T(8,128)S(1)}, f32[1,64,512]{2,1,0:T(8,128)}, u32[]{:S(2)}) copy-start(f32[1,64,512]{2,1,0:T(8,128)} %param.9) | copy-start | bytes 393220
  82.9 4.8 %copy-start.3 = (s32[1,1536]{1,0:T(1,128)S(1)}, s32[1,1536]{1,0:T(1,128)}, u32[]{:S(2)}) copy-start(s32[1,1536]{1,0:T(1,128)} %param.11) | copy-start | bytes 18436
  85.7 217.4 %all-gather.7.cloned.1.call-start = ((), (), s32[]{:S(2)}) async-start(), calls=%async_computation.2 | async-start | bytes 11796480 | tf_op jit(solution)/shard_map/all_gather | solution.py:37
  367.5 18.6 %copy-start.4 = (f32[1,1536]{1,0:T(1,128)S(1)}, f32[1,1536]{1,0:T(1,128)}, u32[]{:S(2)}) copy-start(f32[1,1536]{1,0:T(1,128)} %param.13) | copy-start | bytes 18436
Sparse Core Ops, SparseCore 0:
  9.5 19.4 all-gather.4
  31.1 49.0 all-gather.8
  85.8 62.6 reduce-scatter.3
  150.5 152.4 all-gather.6
where the time goes:
time: 394 us; the launch traced here: 393 us
  waiting for transfers between devices  232 us (59%)
  local copies, waits for them, and re-layouts  75 us (19%)
  blocking collectives  33.3 us (8%)
  matrix products  22.7 us (6%)
  other arithmetic  15.5 us (4%)
  between operations  14.6 us (4%)
    all_gather x1, waiting for transfers between devices, shards(): lax.all_gather(upper_own, 'sub', axis=0, tiled=True)  98.6 us
    unnamed x5, waiting for transfers between devices  61.9 us
    all_gather x1, waiting for transfers between devices, shards(): lax.all_gather(factor, 'sub', axis=0, tiled=True)  51.3 us
    gather x2, local copies, waits for them, and re-layouts, shards(): picked = jnp.take(jnp.take(upper_rows, clipped, axis=0), slot_index, axis=1)  35.1 us
    all_gather x1, blocking collectives, shards(): lax.all_gather(mid_rows, 'sub', axis=0, tiled=True)  33.3 us
    all_gather x1, waiting for transfers between devices, shards(): top_rows = lax.all_gather(g_top, 'sep', axis=1, tiled=True)  20.3 us
    dot_general x1, matrix products, shards(): product = jnp.dot(chosen, masked, preferred_element_type=jnp.float32)  18.6 us
    gather x3, local copies, waits for them, and re-layouts, shards(): mid_mid = jnp.take(jnp.take(whole_block, midpos, axis=0), midpos, axis=1)  17.6 us
  transfers between devices with their start and end apart: 4, of which 4 were waited for; matrix products, arithmetic and copies ran while one was open for 6% of the time, Pallas kernels for 0%

commit v1 on v0

v1 whole, which is shorter than its diff:
```python
import functools
import math

import jax
import jax.numpy as jnp
from jax import lax
from jax.experimental import pallas as pl
from jax.experimental.pallas import tpu as pltpu
from jax.sharding import PartitionSpec as P

MESH = pl.DeviceIdType.MESH
F32 = jnp.float32
BF16 = jnp.bfloat16


def nearest(p, k, n):
    room = jnp.minimum(p, n - 1 - p)
    near = jnp.where(k % 2 == 1, p - (k + 1) // 2, p + k // 2)
    far = jnp.where(p < n - 1 - p, k, n - 1 - k)
    return jnp.where(k <= 2 * room, near, far)


def gather_kernel(nx, ny, nz, g_ref, u_ref, b_ref, g_all, u_all, b_all,
                  own_sem, g_recv, g_peer, g_send, u_recv, u_send, b_recv, b_send):
    sep, sub = lax.axis_index("sep"), lax.axis_index("sub")
    x, core = sep // 2, sep % 2
    z, y = sub // ny, sub % ny
    rows, cols = g_ref.shape
    mid = b_ref.shape[0]

    def device(xx, cc, zz, yy):
        return (xx * 2 + cc, zz * ny + yy)

    def g_block(zz, yy, xx, cc):
        return g_all.at[pl.ds(pl.multiple_of((zz * ny + yy) * rows, rows), rows),
                        pl.ds(pl.multiple_of((xx * 2 + cc) * cols, cols), cols)]

    def u_block(zz, yy):
        return u_all.at[pl.ds(pl.multiple_of((zz * ny + yy) * rows, rows), rows), :]

    def b_block(zz, yy):
        return b_all.at[pl.ds(pl.multiple_of((zz * ny + yy) * mid, mid), mid), :]

    steps = (
        (x > 0, device(x - 1, core, z, y)),
        (x < nx - 1, device(x + 1, core, z, y)),
        (y > 0, device(x, core, z, y - 1)),
        (y < ny - 1, device(x, core, z, y + 1)),
        (z > 0, device(x, core, z - 1, y)),
        (z < nz - 1, device(x, core, z + 1, y)),
        (core >= 0, device(x, 1 - core, z, y)),
    )
    own = (
        pltpu.make_async_copy(g_ref, g_block(z, y, x, core), own_sem.at[0]),
        pltpu.make_async_copy(u_ref, u_block(z, y), own_sem.at[1]),
        pltpu.make_async_copy(b_ref, b_block(z, y), own_sem.at[2]),
    )
    for copy in own:
        copy.start()
    barrier = pltpu.get_barrier_semaphore()
    total = jnp.int32(0)
    for valid, target in steps:
        total = total + valid.astype(jnp.int32)

        @pl.when(valid)
        def _():
            pl.semaphore_signal(barrier, inc=1, device_id=target, device_id_type=MESH)
    pl.semaphore_wait(barrier, total)
    for copy in own:
        copy.wait()

    def send(go, way, block, send_sem, recv_sem, start):
        valid, target = steps[way]

        @pl.when(jnp.logical_and(go, valid))
        def _():
            copy = pltpu.make_async_remote_copy(
                src_ref=block, dst_ref=block, send_sem=send_sem.at[way], recv_sem=recv_sem,
                device_id=target, device_id_type=MESH)
            if start:
                copy.start()
            else:
                copy.wait_send()

    def arrive(block, send_sem, recv_sem):
        pltpu.make_async_remote_copy(
            src_ref=block, dst_ref=block, send_sem=send_sem, recv_sem=recv_sem,
            device_id=steps[6][1], device_id_type=MESH).wait_recv()

    def g_event(zz, yy, xx, start):
        index = (zz * ny + yy) * nx + xx
        block = g_block(zz, yy, xx, core)
        sems = g_send.at[index]
        if start:
            @pl.when(jnp.logical_or(xx != x, jnp.logical_or(yy != y, zz != z)))
            def _():
                arrive(block, sems.at[0], g_recv.at[index])
        in_x = xx == x
        in_xy = jnp.logical_and(in_x, yy == y)
        go = functools.partial(send, block=block, send_sem=sems, recv_sem=g_recv.at[index], start=start)
        go(xx >= x, 0)
        go(xx <= x, 1)
        go(jnp.logical_and(in_x, yy >= y), 2)
        go(jnp.logical_and(in_x, yy <= y), 3)
        go(jnp.logical_and(in_xy, zz >= z), 4)
        go(jnp.logical_and(in_xy, zz <= z), 5)
        send(core >= 0, 6, block, sems, g_peer.at[index], start)

    def u_event(zz, yy, start):
        index = zz * ny + yy
        block = u_block(zz, yy)
        sems = u_send.at[index]
        if start:
            @pl.when(jnp.logical_or(yy != y, zz != z))
            def _():
                arrive(block, sems.at[0], u_recv.at[index])
        in_y = yy == y
        go = functools.partial(send, block=block, send_sem=sems, recv_sem=u_recv.at[index], start=start)
        go(yy >= y, 2)
        go(yy <= y, 3)
        go(jnp.logical_and(in_y, zz >= z), 4)
        go(jnp.logical_and(in_y, zz <= z), 5)

    def b_event(zz, yy, start):
        index = zz * ny + yy
        block = b_block(zz, yy)
        sems = b_send.at[index]
        if start:
            @pl.when(jnp.logical_or(yy != y, zz != z))
            def _():
                arrive(block, sems.at[0], b_recv.at[index])
        in_z = zz == z
        go = functools.partial(send, block=block, send_sem=sems, recv_sem=b_recv.at[index], start=start)
        go(jnp.logical_and(in_z, yy >= y), 2)
        go(jnp.logical_and(in_z, yy <= y), 3)
        go(zz >= z, 4)
        go(zz <= z, 5)

    def over_y(body):
        def run(k, carry):
            body(nearest(y, k, ny))
            return carry
        lax.fori_loop(0, ny, run, 0)

    def over_x(first, body):
        def run(k, carry):
            body(nearest(x, k, nx))
            return carry
        lax.fori_loop(first, nx, run, 0)

    def group(k, carry):
        @pl.when(k < nz)
        def _():
            zz = nearest(z, k, nz)
            over_y(lambda yy: g_event(zz, yy, x, True))
            over_y(lambda yy: u_event(zz, yy, True))
            over_y(lambda yy: b_event(zz, yy, True))

        @pl.when(k > 0)
        def _():
            zz = nearest(z, k - 1, nz)
            over_y(lambda yy: over_x(1, lambda xx: g_event(zz, yy, xx, True)))
        return carry

    lax.fori_loop(0, nz + 1, group, 0)

    def finish(zz, carry):
        def inner(yy, carry):
            u_event(zz, yy, False)
            b_event(zz, yy, False)

            def last(xx, carry):
                g_event(zz, yy, xx, False)
                index = (zz * ny + yy) * nx + xx
                arrive(g_block(zz, yy, xx, 1 - core), g_send.at[index].at[6], g_peer.at[index])
                return carry
            return lax.fori_loop(0, nx, last, carry)
        return lax.fori_loop(0, ny, inner, carry)

    lax.fori_loop(0, nz, finish, 0)


def gather_all(n_sep, n_sub, g_top, u_mid, b_mid):
    nx = n_sep // 2
    ny = math.isqrt(n_sub // 2)
    nz = n_sub // ny
    order = g_top.shape[0] * n_sub
    dma = pltpu.SemaphoreType.DMA
    n = nx * n_sub
    any_space = pl.BlockSpec(memory_space=pl.ANY)
    vmem = pl.BlockSpec(memory_space=pltpu.VMEM)
    return pl.pallas_call(
        functools.partial(gather_kernel, nx, ny, nz),
        out_shape=(
            jax.ShapeDtypeStruct((order, order), g_top.dtype),
            jax.ShapeDtypeStruct((order, u_mid.shape[1]), u_mid.dtype),
            jax.ShapeDtypeStruct((b_mid.shape[0] * n_sub, b_mid.shape[1]), b_mid.dtype),
        ),
        in_specs=[vmem] * 3,
        out_specs=(any_space,) * 3,
        scratch_shapes=[
            dma((3,)), dma((n,)), dma((n,)), dma((n, 7)),
            dma((n_sub,)), dma((n_sub, 7)), dma((n_sub,)), dma((n_sub, 7)),
        ],
        compiler_params=pltpu.CompilerParams(collective_id=0, has_side_effects=True),
    )(g_top, u_mid, b_mid)


def leaf_kernel(top, g_ref, cross_ref, cross_t_ref, mid_ref, across_ref, down_ref, bdiag_ref, u_ref,
                off_ref, diag_ref, pick, place):
    @pl.when(pl.program_id(0) == 0)
    def _():
        step = 256

        @pl.loop(0, place.shape[0] // step)
        def _(i):
            at = pl.multiple_of(i * step, step)
            row = lax.broadcasted_iota(jnp.int32, (step, place.shape[1]), 0) + at
            place[pl.ds(at, step), :] = jnp.where(row == across_ref[...], 1.0, 0.0).astype(BF16)

        @pl.loop(0, pick.shape[0] // step)
        def _(i):
            at = pl.multiple_of(i * step, step)
            column = lax.broadcasted_iota(jnp.int32, (step, pick.shape[1]), 1)
            pick[pl.ds(at, step), :] = jnp.where(column == down_ref[pl.ds(at, step), :], 1.0, 0.0).astype(BF16)

    dot = functools.partial(jnp.dot, preferred_element_type=F32)
    spread = dot(place[...], u_ref[...]).astype(BF16)
    upper, lower = spread[:top], spread[top:]
    high = dot(g_ref[...], upper) + dot(cross_ref[...], lower)
    low = dot(cross_t_ref[...], upper) + dot(mid_ref[...], lower)
    diag_ref[...] = (bdiag_ref[...]
                     + jnp.sum(upper.astype(F32) * high, axis=0, keepdims=True)
                     + jnp.sum(lower.astype(F32) * low, axis=0, keepdims=True))
    picked = dot(pick[:, :top], (-high).astype(BF16)) + dot(pick[:, top:], (-low).astype(BF16))
    off_ref[...] = picked.astype(BF16)


def leaf(g_all, cross, mid, slot_index, u_leaf, bdiag):
    top, wide = cross.shape
    slots, columns = u_leaf.shape
    total = top + wide
    tile = 256
    once = pl.Buffered(1)

    def whole(shape):
        return pl.BlockSpec(shape, lambda j: (0,) * len(shape), pipeline_mode=once)
    return pl.pallas_call(
        functools.partial(leaf_kernel, top),
        grid=(columns // tile,),
        out_shape=(jax.ShapeDtypeStruct((slots, columns), BF16),
                   jax.ShapeDtypeStruct((1, columns), F32)),
        in_specs=[
            whole((top, top)), whole((top, wide)), whole((wide, top)), whole((wide, wide)),
            whole((1, slots)), whole((slots, 1)),
            pl.BlockSpec((1, tile), lambda j: (0, j)),
            pl.BlockSpec((slots, tile), lambda j: (0, j)),
        ],
        out_specs=(pl.BlockSpec((slots, tile), lambda j: (0, j)),
                   pl.BlockSpec((1, tile), lambda j: (0, j))),
        scratch_shapes=[pltpu.VMEM((slots, total), BF16), pltpu.VMEM((total, slots), BF16)],
        compiler_params=pltpu.CompilerParams(vmem_limit_bytes=60 * 2**20),
    )(g_all, cross, cross.T, mid, slot_index[None, :], slot_index[:, None], bdiag[None, :], u_leaf)


def shards(n_sep, n_sub, g_top, u_mid, b_mid, u_leaf, leaf_index, leaf_count, leaf_bdiag):
    rows, mid = u_mid.shape[1], b_mid.shape[1]
    g_all, u_all, b_all = gather_all(n_sep, n_sub, g_top, u_mid[0], b_mid[0])
    cross = (-jnp.dot(g_all, u_all, preferred_element_type=F32)).astype(BF16)
    projected = lax.dot_general(u_all, cross, (((0,), (0,)), ((), ())), preferred_element_type=F32)
    block = (b_all - projected).astype(BF16)
    me = lax.axis_index("sub")
    cross_rows = lax.dynamic_slice_in_dim(cross, me * rows, rows, 0)
    mid_rows = lax.dynamic_slice_in_dim(block, me * mid, mid, 0)
    slots = leaf_index.shape[1]
    live = jnp.arange(slots, dtype=jnp.int32) < leaf_count[0]
    slot_index = jnp.where(live, leaf_index[0], -1)
    off, diag = leaf(g_all, cross, block, slot_index, u_leaf[0], leaf_bdiag[0])
    return cross_rows[None], mid_rows[None], off[None], diag


def solution(mesh):
    return jax.shard_map(
        functools.partial(shards, mesh.shape["sep"], mesh.shape["sub"]),
        mesh=mesh,
        in_specs=(
            P("sub", "sep"),
            P("sep", "sub", None),
            P("sep", "sub", None),
            P(("sep", "sub"), None, None),
            P(("sep", "sub"), None),
            P(("sep", "sub")),
            P(("sep", "sub"), None),
        ),
        out_specs=(
            P("sep", "sub", None),
            P("sep", "sub", None),
            P(("sep", "sub"), None, None),
            P(("sep", "sub"), None),
        ),
        check_vma=False,
    )
```

time: 394 us -> 177 us (0.45)
  waiting for transfers between devices: 232 us -> 0 us
  Pallas kernels: 0 us -> 157 us
  local copies, waits for them, and re-layouts: 75 us -> 6.09 us
  blocking collectives: 33.3 us -> 0 us
  other arithmetic: 15.5 us -> 1.62 us
  between operations: 14.6 us -> 1.36 us
  matrix products: 22.7 us -> 10.8 us
    all_gather x3 -> x0, waiting for transfers between devices: 170 us -> none  [the longest x1 98.6 us: shards(): lax.all_gather(upper_own, 'sub', axis=0, tiled=True)]
    pallas_call x0 -> x2, Pallas kernels: none -> 157 us  [the longest x1 83.3 us: gather_all(): pl.pallas_call(functools.partial(gather_kernel, nx, ny, nz), out_shape=(j...]
    unnamed x5 -> x0, waiting for transfers between devices: 61.9 us -> none
    gather x5 -> x0, local copies, waits for them, and re-layouts: 52.7 us -> none  [the longest x2 35.1 us: shards(): picked = jnp.take(jnp.take(upper_rows, clipped, axis=0), slot_index, axis=1)]
    all_gather x1 -> x0, blocking collectives: 33.3 us -> none  [shards(): lax.all_gather(mid_rows, 'sub', axis=0, tiled=True)]
    select_n x3 -> x0, local copies, waits for them, and re-layouts: 19 us -> none  [the longest x2 17.3 us: shards(): picked = jnp.take(jnp.take(upper_rows, clipped, axis=0), slot_index, axis=1)]
    select_n x3 -> x2, other arithmetic: 13.5 us -> 1.62 us  [shards(): slot_index = jnp.where(live, leaf_index[0], -1)]
    dot_general x3 -> x2, matrix products: 22.7 us -> 10.8 us  [the longest x1 8.7 us: shards(): cross = (-jnp.dot(g_all, u_all, preferred_element_type=F32)).astype(BF16)]
  transfers between devices with their start and end apart: 4 -> 0, of which waited for: 4 -> 0; matrix products, arithmetic and copies ran while one was open for 6% -> 0% of each run, Pallas kernels for 0% -> 0%
where the time goes in v1:
time: 177 us
  Pallas kernels  157 us (89%)
  matrix products  10.8 us (6%)
  local copies, waits for them, and re-layouts  6.09 us (3%)
    pallas_call x1, Pallas kernels, gather_all(): pl.pallas_call(functools.partial(gather_kernel, nx, ny, nz), out_shape=(j...  83.3 us
    pallas_call x1, Pallas kernels, leaf(): pl.pallas_call(functools.partial(leaf_kernel, top), grid=(columns // tile...  73.5 us
    dot_general x1, matrix products, shards(): cross = (-jnp.dot(g_all, u_all, preferred_element_type=F32)).astype(BF16)  8.7 us

profile of v1, /device:TPU:0, one launch (start us, length us, event | category | flops | bytes accessed | tf_op | source)
XLA Modules:
  0.0 176.7 jit_solution(9860453571450329577)
XLA Ops:
  0.6 83.3 %shard_map.102 = (bf16[2048,2048]{1,0:T(8,128)(2,1)}, bf16[2048,512]{1,0:T(8,128)(2,1)}, f32[512,512]{1,0:T(8,128)}) custom-call(bf16[256,512]{1,0:T(8,128)(2,1)} %g_ref.1, bf16[256,512]{1,0:T(8,128)(2,1)} %bitcast.18, f32[64,512]{1,0:T(8,128)} %bitcast.20), custom_call_target="tpu_custom_call" | custom-call | tf_op jit(solution)/shard_map/pallas_call | solution.py:192
  83.9 0.0 copy-start.2
  83.9 0.0 copy-start.3
  83.9 8.7 %negate_convert_fusion = bf16[2048,512]{0,1:T(8,128)(2,1)S(1)} fusion(bf16[2048,2048]{1,0:T(8,128)(2,1)} %get-tuple-element.9.g_ref, bf16[2048,512]{1,0:T(8,128)(2,1)} %get-tuple-element.10), kind=kOutput, calls=%fused_computation | convolution fusion | flops 4297064448 | bytes 12582912 | tf_op jit(solution)/shard_map/dot_general | solution.py:269
  92.6 0.0 copy-start
  92.6 0.0 copy-done.2
  92.7 0.0 copy-done.3
  92.7 2.1 %fusion.mid_ref = bf16[512,512]{1,0:T(8,128)(2,1)} fusion(f32[512,512]{1,0:T(8,128)S(1)} %copy-done.3, bf16[2048,512]{1,0:T(8,128)(2,1)S(1)} %copy-done.2, bf16[2048,512]{0,1:T(8,128)(2,1)S(1)} %negate_convert_fusion), kind=kOutput, calls=%fused_computation.2 | convolution fusion | flops 1074266112 | bytes 5767168 | tf_op jit(solution)/shard_map/dot_general | solution.py:270
  94.8 0.0 copy-done
  94.8 0.0 copy-start.1
  94.8 2.5 %copy.16.cross_ref = bf16[2048,512]{1,0:T(8,128)(2,1)} copy(bf16[2048,512]{0,1:T(8,128)(2,1)S(1)} %negate_convert_fusion) | data formatting | bytes 4194304 | tf_op jit(solution)/shard_map/convert_element_type | solution.py:269
  97.9 0.0 copy-done.1
  97.9 0.3 copy.15
  98.2 1.0 fusion.1.down_ref
  99.2 0.6 compare_select_fusion.across_ref
  99.8 73.5 %shard_map.103 = (bf16[1536,1536]{1,0:T(8,128)(2,1)}, f32[1,1536]{1,0:T(1,128)}) custom-call(bf16[2048,2048]{1,0:T(8,128)(2,1)} %get-tuple-element.9.g_ref, bf16[2048,512]{1,0:T(8,128)(2,1)} %copy.16.cross_ref, bf16[512,2048]{1,0:T(8,128)(2,1)} %bitcast.16, bf16[512,512]{1,0:T(8,128)(2,1)} %fusion.mid_ref, s32[1,1536]{1,0:T(1,128)} %compare_select_fusion.across_ref, ...), custom_call_target="tpu_custom_call" | custom-call | tf_op jit(solution)/shard_map/pallas_call | solution.py:248
  173.4 1.5 dynamic-slice_bitcast_fusion
  174.9 1.0 constant_dynamic-slice_fusion
  175.8 0.8 copy.14
Async XLA Ops:
  83.9 8.7 %copy-start.2 = (bf16[2048,512]{1,0:T(8,128)(2,1)S(1)}, bf16[2048,512]{1,0:T(8,128)(2,1)}, u32[]{:S(2)}) copy-start(bf16[2048,512]{1,0:T(8,128)(2,1)} %get-tuple-element.10) | copy-start | bytes 6291460
  83.9 8.7 %copy-start.3 = (f32[512,512]{1,0:T(8,128)S(1)}, f32[512,512]{1,0:T(8,128)}, u32[]{:S(2)}) copy-start(f32[512,512]{1,0:T(8,128)} %get-tuple-element.11) | copy-start | bytes 3145732
  92.6 2.1 %copy-start = (bf16[2048,512]{0,1:T(8,128)(2,1)}, bf16[2048,512]{0,1:T(8,128)(2,1)S(1)}, u32[]{:S(2)}) copy-start(bf16[2048,512]{0,1:T(8,128)(2,1)S(1)} %negate_convert_fusion) | copy-start | bytes 6291460
  94.8 3.2 %copy-start.1 = (s32[1,1536]{1,0:T(1,128)S(1)}, s32[1,1536]{1,0:T(1,128)}, u32[]{:S(2)}) copy-start(s32[1,1536]{1,0:T(1,128)} %param.11) | copy-start | bytes 18436

commit v2 on v1

--- a/solution.py
+++ b/solution.py
@@ -20,7 +20,9 @@
     return jnp.where(k <= 2 * room, near, far)
 
 
-def gather_kernel(nx, ny, nz, g_ref, u_ref, b_ref, g_all, u_all, b_all,
+def gather_kernel(nx, ny, nz, g_ref, u_ref, b_ref, across_ref, bdiag_ref, leaf_ref,
+                  cross_out, mid_out, y_ref, diag_ref,
+                  g_all, u_all, b_all, leaf_all, spread, low, projected, block,
                   own_sem, g_recv, g_peer, g_send, u_recv, u_send, b_recv, b_send):
     sep, sub = lax.axis_index("sep"), lax.axis_index("sub")
     x, core = sep // 2, sep % 2
@@ -55,8 +57,10 @@
         pltpu.make_async_copy(u_ref, u_block(z, y), own_sem.at[1]),
         pltpu.make_async_copy(b_ref, b_block(z, y), own_sem.at[2]),
     )
+    leaf_copy = pltpu.make_async_copy(leaf_ref, leaf_all, own_sem.at[3])
     for copy in own:
         copy.start()
+    leaf_copy.start()
     barrier = pltpu.get_barrier_semaphore()
     total = jnp.int32(0)
     for valid, target in steps:
@@ -148,21 +152,105 @@
             return carry
         lax.fori_loop(first, nx, run, 0)
 
+    top, wide = u_all.shape
+    chunk = 256
+    half = spread.shape[0] // chunk // 2
+    tile = 512
+    dot = functools.partial(jnp.dot, preferred_element_type=F32)
+    dot_t = functools.partial(lax.dot_general, dimension_numbers=(((0,), (0,)), ((), ())),
+                              preferred_element_type=F32)
+
+    def place(first, last):
+        @pl.loop(first, last)
+        def _(i):
+            at = pl.multiple_of(i * chunk, chunk)
+            row = lax.broadcasted_iota(jnp.int32, (chunk, across_ref.shape[1]), 0) + at
+            one_hot = jnp.where(row == across_ref[...], 1.0, 0.0).astype(BF16)
+            spread[pl.ds(at, chunk), :] = dot(one_hot, leaf_all[...]).astype(BF16)
+
+    def add_diag(part, product, span):
+        diag_ref[:, span] += jnp.sum(part.astype(F32) * product, axis=0, keepdims=True)
+
+    def compute(zz, yy):
+        at = pl.ds(pl.multiple_of((zz * ny + yy) * rows, rows), rows)
+        cross = (-dot(g_all[at, :], u_all[...])).astype(BF16)
+
+        @pl.when(jnp.logical_and(zz == z, yy == y))
+        def _():
+            cross_out[...] = cross
+        projected[...] += dot_t(u_all[at, :], cross)
+
+        @pl.loop(0, y_ref.shape[1] // tile)
+        def _(j):
+            span = pl.ds(pl.multiple_of(j * tile, tile), tile)
+            own_part = spread[at, span]
+            product = dot(g_all[at, :], spread[:top, span]) + dot(cross, spread[top:, span])
+            y_ref[at, span] = (-product).astype(BF16)
+            add_diag(own_part, product, span)
+            low[:, span] += dot_t(cross, own_part)
+
+    projected[...] = jnp.zeros_like(projected)
+    low[...] = jnp.zeros_like(low)
+    diag_ref[...] = bdiag_ref[...]
+
     def group(k, carry):
         @pl.when(k < nz)
         def _():
             zz = nearest(z, k, nz)
             over_y(lambda yy: g_event(zz, yy, x, True))
-            over_y(lambda yy: u_event(zz, yy, True))
-            over_y(lambda yy: b_event(zz, yy, True))
-
-        @pl.when(k > 0)
+
+        @pl.when(k == 0)
+        def _():
+            over_y(lambda yy: u_event(nearest(z, 0, nz), yy, True))
+            leaf_copy.wait()
+            place(0, half)
+            over_y(lambda yy: u_event(nearest(z, 1, nz), yy, True))
+
+        @pl.when(k == 1)
+        def _():
+            over_y(lambda yy: u_event(nearest(z, 2, nz), yy, True))
+            place(half, 2 * half)
+
+            def rest(i, carry):
+                over_y(lambda yy: u_event(nearest(z, i, nz), yy, True))
+                return carry
+            lax.fori_loop(3, nz, rest, 0)
+
+        @pl.when(k < nz)
+        def _():
+            over_y(lambda yy: b_event(nearest(z, k, nz), yy, True))
+
+        @pl.when(k > 1)
+        def _():
+            zz = nearest(z, k - 2, nz)
+
+            def rows_of(yy):
+                def peer(xx, carry):
+                    index = (zz * ny + yy) * nx + xx
+                    arrive(g_block(zz, yy, xx, 1 - core), g_send.at[index].at[6], g_peer.at[index])
+                    return carry
+                lax.fori_loop(0, nx, peer, 0)
+                compute(zz, yy)
+            over_y(rows_of)
+
+        @pl.when(jnp.logical_and(k > 0, k <= nz))
         def _():
             zz = nearest(z, k - 1, nz)
             over_y(lambda yy: over_x(1, lambda xx: g_event(zz, yy, xx, True)))
         return carry
 
-    lax.fori_loop(0, nz + 1, group, 0)
+    lax.fori_loop(0, nz + 2, group, 0)
+
+    block[...] = (b_all[...] - projected[...]).astype(BF16)
+    mid_out[...] = block[pl.ds(pl.multiple_of((z * ny + y) * mid, mid), mid), :]
+
+    @pl.loop(0, y_ref.shape[1] // tile)
+    def _(j):
+        span = pl.ds(pl.multiple_of(j * tile, tile), tile)
+        part = spread[top:, span]
+        product = low[:, span] + dot(block[...], part)
+        y_ref[top:, span] = (-product).astype(BF16)
+        add_diag(part, product, span)
 
     def finish(zz, carry):
         def inner(yy, carry):
@@ -171,8 +259,6 @@
 
             def last(xx, carry):
                 g_event(zz, yy, xx, False)
-                index = (zz * ny + yy) * nx + xx
-                arrive(g_block(zz, yy, xx, 1 - core), g_send.at[index].at[6], g_peer.at[index])
                 return carry
             return lax.fori_loop(0, nx, last, carry)
         return lax.fori_loop(0, ny, inner, carry)
@@ -180,11 +266,13 @@
     lax.fori_loop(0, nz, finish, 0)
 
 
-def gather_all(n_sep, n_sub, g_top, u_mid, b_mid):
+def gather_all(n_sep, n_sub, g_top, u_mid, b_mid, across, bdiag, u_leaf):
     nx = n_sep // 2
     ny = math.isqrt(n_sub // 2)
     nz = n_sub // ny
-    order = g_top.shape[0] * n_sub
+    top = g_top.shape[0] * n_sub
+    wide = u_mid.shape[1]
+    slots, columns = u_leaf.shape
     dma = pltpu.SemaphoreType.DMA
     n = nx * n_sub
     any_space = pl.BlockSpec(memory_space=pl.ANY)
@@ -192,90 +280,54 @@
     return pl.pallas_call(
         functools.partial(gather_kernel, nx, ny, nz),
         out_shape=(
-            jax.ShapeDtypeStruct((order, order), g_top.dtype),
-            jax.ShapeDtypeStruct((order, u_mid.shape[1]), u_mid.dtype),
-            jax.ShapeDtypeStruct((b_mid.shape[0] * n_sub, b_mid.shape[1]), b_mid.dtype),
+            jax.ShapeDtypeStruct(u_mid.shape, BF16),
+            jax.ShapeDtypeStruct(b_mid.shape, BF16),
+            jax.ShapeDtypeStruct((top + wide, columns), BF16),
+            jax.ShapeDtypeStruct((1, columns), F32),
         ),
-        in_specs=[vmem] * 3,
-        out_specs=(any_space,) * 3,
+        in_specs=[any_space] * 3 + [vmem] * 2 + [any_space],
+        out_specs=(vmem,) * 4,
         scratch_shapes=[
-            dma((3,)), dma((n,)), dma((n,)), dma((n, 7)),
+            pltpu.VMEM((top, top), BF16), pltpu.VMEM((top, wide), BF16), pltpu.VMEM((wide, wide), F32),
+            pltpu.VMEM((slots, columns), BF16), pltpu.VMEM((top + wide, columns), BF16),
+            pltpu.VMEM((wide, columns), F32), pltpu.VMEM((wide, wide), F32), pltpu.VMEM((wide, wide), BF16),
+            dma((4,)), dma((n,)), dma((n,)), dma((n, 7)),
             dma((n_sub,)), dma((n_sub, 7)), dma((n_sub,)), dma((n_sub, 7)),
         ],
-        compiler_params=pltpu.CompilerParams(collective_id=0, has_side_effects=True),
-    )(g_top, u_mid, b_mid)
-
-
-def leaf_kernel(top, g_ref, cross_ref, cross_t_ref, mid_ref, across_ref, down_ref, bdiag_ref, u_ref,
-                off_ref, diag_ref, pick, place):
-    @pl.when(pl.program_id(0) == 0)
-    def _():
-        step = 256
-
-        @pl.loop(0, place.shape[0] // step)
-        def _(i):
-            at = pl.multiple_of(i * step, step)
-            row = lax.broadcasted_iota(jnp.int32, (step, place.shape[1]), 0) + at
-            place[pl.ds(at, step), :] = jnp.where(row == across_ref[...], 1.0, 0.0).astype(BF16)
-
-        @pl.loop(0, pick.shape[0] // step)
-        def _(i):
-            at = pl.multiple_of(i * step, step)
-            column = lax.broadcasted_iota(jnp.int32, (step, pick.shape[1]), 1)
-            pick[pl.ds(at, step), :] = jnp.where(column == down_ref[pl.ds(at, step), :], 1.0, 0.0).astype(BF16)
-
-    dot = functools.partial(jnp.dot, preferred_element_type=F32)
-    spread = dot(place[...], u_ref[...]).astype(BF16)
-    upper, lower = spread[:top], spread[top:]
-    high = dot(g_ref[...], upper) + dot(cross_ref[...], lower)
-    low = dot(cross_t_ref[...], upper) + dot(mid_ref[...], lower)
-    diag_ref[...] = (bdiag_ref[...]
-                     + jnp.sum(upper.astype(F32) * high, axis=0, keepdims=True)
-                     + jnp.sum(lower.astype(F32) * low, axis=0, keepdims=True))
-    picked = dot(pick[:, :top], (-high).astype(BF16)) + dot(pick[:, top:], (-low).astype(BF16))
-    off_ref[...] = picked.astype(BF16)
-
-
-def leaf(g_all, cross, mid, slot_index, u_leaf, bdiag):
-    top, wide = cross.shape
-    slots, columns = u_leaf.shape
-    total = top + wide
+        compiler_params=pltpu.CompilerParams(collective_id=0, has_side_effects=True,
+                                             vmem_limit_bytes=60 * 2**20),
+    )(g_top, u_mid, b_mid, across, bdiag, u_leaf)
+
+
+def pick_kernel(down_ref, y_ref, off_ref):
+    column = lax.broadcasted_iota(jnp.int32, (off_ref.shape[0], y_ref.shape[0]), 1)
+    pick = jnp.where(column == down_ref[...], 1.0, 0.0).astype(BF16)
+    off_ref[...] = jnp.dot(pick, y_ref[...], preferred_element_type=F32).astype(BF16)
+
+
+def pick_rows(down, y):
+    slots, (total, columns) = down.shape[0], y.shape
     tile = 256
-    once = pl.Buffered(1)
-
-    def whole(shape):
-        return pl.BlockSpec(shape, lambda j: (0,) * len(shape), pipeline_mode=once)
     return pl.pallas_call(
-        functools.partial(leaf_kernel, top),
-        grid=(columns // tile,),
-        out_shape=(jax.ShapeDtypeStruct((slots, columns), BF16),
-                   jax.ShapeDtypeStruct((1, columns), F32)),
+        pick_kernel,
+        grid=(slots // tile,),
+        out_shape=jax.ShapeDtypeStruct((slots, columns), BF16),
         in_specs=[
-            whole((top, top)), whole((top, wide)), whole((wide, top)), whole((wide, wide)),
-            whole((1, slots)), whole((slots, 1)),
-            pl.BlockSpec((1, tile), lambda j: (0, j)),
-            pl.BlockSpec((slots, tile), lambda j: (0, j)),
+            pl.BlockSpec((tile, 1), lambda i: (i, 0)),
+            pl.BlockSpec((total, columns), lambda i: (0, 0), pipeline_mode=pl.Buffered(1)),
         ],
-        out_specs=(pl.BlockSpec((slots, tile), lambda j: (0, j)),
-                   pl.BlockSpec((1, tile), lambda j: (0, j))),
-        scratch_shapes=[pltpu.VMEM((slots, total), BF16), pltpu.VMEM((total, slots), BF16)],
-        compiler_params=pltpu.CompilerParams(vmem_limit_bytes=60 * 2**20),
-    )(g_all, cross, cross.T, mid, slot_index[None, :], slot_index[:, None], bdiag[None, :], u_leaf)
+        out_specs=pl.BlockSpec((tile, columns), lambda i: (i, 0)),
+        compiler_params=pltpu.CompilerParams(vmem_limit_bytes=40 * 2**20),
+    )(down, y)
 
 
 def shards(n_sep, n_sub, g_top, u_mid, b_mid, u_leaf, leaf_index, leaf_count, leaf_bdiag):
-    rows, mid = u_mid.shape[1], b_mid.shape[1]
-    g_all, u_all, b_all = gather_all(n_sep, n_sub, g_top, u_mid[0], b_mid[0])
-    cross = (-jnp.dot(g_all, u_all, preferred_element_type=F32)).astype(BF16)
-    projected = lax.dot_general(u_all, cross, (((0,), (0,)), ((), ())), preferred_element_type=F32)
-    block = (b_all - projected).astype(BF16)
-    me = lax.axis_index("sub")
-    cross_rows = lax.dynamic_slice_in_dim(cross, me * rows, rows, 0)
-    mid_rows = lax.dynamic_slice_in_dim(block, me * mid, mid, 0)
     slots = leaf_index.shape[1]
-    live = jnp.arange(slots, dtype=jnp.int32) < leaf_count[0]
-    slot_index = jnp.where(live, leaf_index[0], -1)
-    off, diag = leaf(g_all, cross, block, slot_index, u_leaf[0], leaf_bdiag[0])
+    live = jnp.arange(slots, dtype=jnp.int32)[None, :] < leaf_count[0]
+    across = jnp.where(live, leaf_index, -1)
+    cross_rows, mid_rows, y, diag = gather_all(
+        n_sep, n_sub, g_top, u_mid[0], b_mid[0], across, leaf_bdiag, u_leaf[0])
+    off = pick_rows(across.reshape(slots, 1), y)
     return cross_rows[None], mid_rows[None], off[None], diag
 
 

time: 177 us -> 150 us (0.85)
  Pallas kernels: 157 us -> 141 us
  matrix products: 10.8 us -> 0 us
    pallas_call x1, Pallas kernels: 73.5 us -> 14.3 us  [pick_rows(): pl.pallas_call(pick_kernel, grid=(slots // tile,), out_shape=jax.ShapeDty...]
    pallas_call x1, Pallas kernels: 83.3 us -> 127 us  [gather_all(): pl.pallas_call(functools.partial(gather_kernel, nx, ny, nz), out_shape=(j...]
    dot_general x2 -> x0, matrix products: 10.8 us -> none  [the longest x1 8.7 us: shards(): cross = (-jnp.dot(g_all, u_all, preferred_element_type=F32)).astype(BF16)]
    unnamed x8 -> x11, local copies, waits for them, and re-layouts: 0.02 us -> 5.16 us
    convert_element_type x1 -> x0, local copies, waits for them, and re-layouts: 2.49 us -> none  [shards(): cross = (-jnp.dot(g_all, u_all, preferred_element_type=F32)).astype(BF16)]
    dynamic_slice x2 -> x0, local copies, waits for them, and re-layouts: 1.81 us -> none  [shards(): cross_rows = lax.dynamic_slice_in_dim(cross, me * rows, rows, 0)]
where the time goes in v2:
time: 150 us
  Pallas kernels  141 us (94%)
  local copies, waits for them, and re-layouts  5.45 us (4%)
  other arithmetic  2 us (1%)
    pallas_call x1, Pallas kernels, gather_all(): pl.pallas_call(functools.partial(gather_kernel, nx, ny, nz), out_shape=(j...  127 us
    pallas_call x1, Pallas kernels, pick_rows(): pl.pallas_call(pick_kernel, grid=(slots // tile,), out_shape=jax.ShapeDty...  14.3 us
    unnamed x11, local copies, waits for them, and re-layouts  5.16 us

profile of v2, /device:TPU:0, one launch (start us, length us, event | category | flops | bytes accessed | tf_op | source)
XLA Modules:
  0.0 149.7 jit_solution(7844655357363536662)
XLA Ops:
  1.3 0.7 fusion
  2.0 1.3 compare_select_fusion.across_ref
  3.3 0.3 copy.11.down_ref
  3.6 126.6 %shard_map.102 = (bf16[256,512]{1,0:T(8,128)(2,1)}, bf16[64,512]{1,0:T(8,128)(2,1)}, bf16[2560,1536]{1,0:T(8,128)(2,1)}, f32[1,1536]{1,0:T(1,128)}) custom-call(bf16[256,512]{1,0:T(8,128)(2,1)} %g_ref.1, bf16[256,512]{1,0:T(8,128)(2,1)} %bitcast.13, f32[64,512]{1,0:T(8,128)} %bitcast.15, s32[1,1536]{1,0:T(1,128)} %compare_select_fusion.across_ref, ...), custom_call_target="tpu_custom_call" | custom-call | tf_op jit(solution)/shard_map/pallas_call | solution.py:280
  130.2 0.0 copy-start
  130.2 3.2 %copy-done = bf16[2560,1536]{1,0:T(8,128)(2,1)S(1)} copy-done((bf16[2560,1536]{1,0:T(8,128)(2,1)S(1)}, bf16[2560,1536]{1,0:T(8,128)(2,1)}, u32[]{:S(2)}) %copy-start) | copy-done | bytes 7864344
  133.4 0.0 copy-start.1
  133.4 0.0 copy-start.2
  133.4 0.0 copy-start.3
  133.4 14.3 %shard_map.103 = bf16[1536,1536]{1,0:T(8,128)(2,1)} custom-call(s32[1536,1]{1,0:T(8,128)S(1)} %copy.11.down_ref, bf16[2560,1536]{1,0:T(8,128)(2,1)S(1)} %copy-done), custom_call_target="tpu_custom_call" | custom-call | tf_op jit(solution)/shard_map/pallas_call | solution.py:311
  147.8 0.0 copy-done.1
  147.8 0.7 copy.16
  148.5 0.0 copy-done.2
  148.5 0.6 copy.17
  149.1 0.0 copy-done.3
  149.1 0.6 copy.18
Async XLA Ops:
  130.2 3.2 %copy-start = (bf16[2560,1536]{1,0:T(8,128)(2,1)S(1)}, bf16[2560,1536]{1,0:T(8,128)(2,1)}, u32[]{:S(2)}) copy-start(bf16[2560,1536]{1,0:T(8,128)(2,1)} %get-tuple-element.10.y_ref) | copy-start | bytes 23592964
  133.4 14.4 %copy-start.1 = (bf16[256,512]{1,0:T(8,128)(2,1)S(1)}, bf16[256,512]{1,0:T(8,128)(2,1)}, u32[]{:S(2)}) copy-start(bf16[256,512]{1,0:T(8,128)(2,1)} %get-tuple-element.8) | copy-start | bytes 786436
  133.4 15.1 %copy-start.2 = (bf16[64,512]{1,0:T(8,128)(2,1)S(1)}, bf16[64,512]{1,0:T(8,128)(2,1)}, u32[]{:S(2)}) copy-start(bf16[64,512]{1,0:T(8,128)(2,1)} %get-tuple-element.9) | copy-start | bytes 196612
  133.4 15.7 %copy-start.3 = (f32[1,1536]{1,0:T(1,128)S(1)}, f32[1,1536]{1,0:T(1,128)}, u32[]{:S(2)}) copy-start(f32[1,1536]{1,0:T(1,128)} %get-tuple-element.19) | copy-start | bytes 18436

commit v3 on v2

--- a/solution.py
+++ b/solution.py
@@ -22,8 +22,8 @@
 
 def gather_kernel(nx, ny, nz, g_ref, u_ref, b_ref, across_ref, bdiag_ref, leaf_ref,
                   cross_out, mid_out, y_ref, diag_ref,
-                  g_all, u_all, b_all, leaf_all, spread, low, projected, block,
-                  own_sem, g_recv, g_peer, g_send, u_recv, u_send, b_recv, b_send):
+                  g_all, u_all, b_all, leaf_all, spread, low, projected, block, crossed,
+                  own_sem, z_send, g_recv, g_peer, g_send, u_recv, u_send, b_recv, b_send):
     sep, sub = lax.axis_index("sep"), lax.axis_index("sub")
     x, core = sep // 2, sep % 2
     z, y = sub // ny, sub % ny
@@ -48,8 +48,6 @@
         (x < nx - 1, device(x + 1, core, z, y)),
         (y > 0, device(x, core, z, y - 1)),
         (y < ny - 1, device(x, core, z, y + 1)),
-        (z > 0, device(x, core, z - 1, y)),
-        (z < nz - 1, device(x, core, z + 1, y)),
         (core >= 0, device(x, 1 - core, z, y)),
     )
     own = (
@@ -62,7 +60,12 @@
         copy.start()
     leaf_copy.start()
     barrier = pltpu.get_barrier_semaphore()
-    total = jnp.int32(0)
+    total = jnp.int32(nz - 1)
+
+    def greet(j, carry):
+        pl.semaphore_signal(barrier, inc=1, device_id=device(x, core, nearest(z, j, nz), y), device_id_type=MESH)
+        return carry
+    lax.fori_loop(1, nz, greet, 0)
     for valid, target in steps:
         total = total + valid.astype(jnp.int32)
 
@@ -89,7 +92,34 @@
     def arrive(block, send_sem, recv_sem):
         pltpu.make_async_remote_copy(
             src_ref=block, dst_ref=block, send_sem=send_sem, recv_sem=recv_sem,
-            device_id=steps[6][1], device_id_type=MESH).wait_recv()
+            device_id=steps[4][1], device_id_type=MESH).wait_recv()
+
+    me = z * ny + y
+    own_blocks = (
+        (g_block(z, y, x, core), g_recv.at[me * nx + x]),
+        (u_block(z, y), u_recv.at[me]),
+        (b_block(z, y), b_recv.at[me]),
+    )
+
+    def column(which, start, near=None):
+        block, recv_sem = own_blocks[which]
+
+        def one(j, carry):
+            zz = nearest(z, j, nz)
+            beside = jnp.logical_or(zz == z - 1, zz == z + 1)
+            wanted = zz >= 0 if near is None else beside if near else jnp.logical_not(beside)
+
+            @pl.when(wanted)
+            def _():
+                copy = pltpu.make_async_remote_copy(
+                    src_ref=block, dst_ref=block, send_sem=z_send.at[which, zz], recv_sem=recv_sem,
+                    device_id=device(x, core, zz, y), device_id_type=MESH)
+                if start:
+                    copy.start()
+                else:
+                    copy.wait_send()
+            return carry
+        lax.fori_loop(1, nz, one, 0)
 
     def g_event(zz, yy, xx, start):
         index = (zz * ny + yy) * nx + xx
@@ -100,51 +130,32 @@
             def _():
                 arrive(block, sems.at[0], g_recv.at[index])
         in_x = xx == x
-        in_xy = jnp.logical_and(in_x, yy == y)
         go = functools.partial(send, block=block, send_sem=sems, recv_sem=g_recv.at[index], start=start)
+        go(jnp.logical_and(in_x, yy >= y), 2)
+        go(jnp.logical_and(in_x, yy <= y), 3)
         go(xx >= x, 0)
         go(xx <= x, 1)
-        go(jnp.logical_and(in_x, yy >= y), 2)
-        go(jnp.logical_and(in_x, yy <= y), 3)
-        go(jnp.logical_and(in_xy, zz >= z), 4)
-        go(jnp.logical_and(in_xy, zz <= z), 5)
-        send(core >= 0, 6, block, sems, g_peer.at[index], start)
-
-    def u_event(zz, yy, start):
+        send(core >= 0, 4, block, sems, g_peer.at[index], start)
+
+    def flat_event(view, send_sems, recv_sems, zz, yy, start):
         index = zz * ny + yy
-        block = u_block(zz, yy)
-        sems = u_send.at[index]
+        block = view(zz, yy)
+        sems = send_sems.at[index]
         if start:
             @pl.when(jnp.logical_or(yy != y, zz != z))
             def _():
-                arrive(block, sems.at[0], u_recv.at[index])
-        in_y = yy == y
-        go = functools.partial(send, block=block, send_sem=sems, recv_sem=u_recv.at[index], start=start)
-        go(yy >= y, 2)
-        go(yy <= y, 3)
-        go(jnp.logical_and(in_y, zz >= z), 4)
-        go(jnp.logical_and(in_y, zz <= z), 5)
-
-    def b_event(zz, yy, start):
-        index = zz * ny + yy
-        block = b_block(zz, yy)
-        sems = b_send.at[index]
-        if start:
-            @pl.when(jnp.logical_or(yy != y, zz != z))
-            def _():
-                arrive(block, sems.at[0], b_recv.at[index])
-        in_z = zz == z
-        go = functools.partial(send, block=block, send_sem=sems, recv_sem=b_recv.at[index], start=start)
-        go(jnp.logical_and(in_z, yy >= y), 2)
-        go(jnp.logical_and(in_z, yy <= y), 3)
-        go(zz >= z, 4)
-        go(zz <= z, 5)
-
-    def over_y(body):
+                arrive(block, sems.at[0], recv_sems.at[index])
+        send(yy >= y, 2, block, sems, recv_sems.at[index], start)
+        send(yy <= y, 3, block, sems, recv_sems.at[index], start)
+
+    u_event = functools.partial(flat_event, u_block, u_send, u_recv)
+    b_event = functools.partial(flat_event, b_block, b_send, b_recv)
+
+    def over_y(body, first=0):
         def run(k, carry):
             body(nearest(y, k, ny))
             return carry
-        lax.fori_loop(0, ny, run, 0)
+        lax.fori_loop(first, ny, run, 0)
 
     def over_x(first, body):
         def run(k, carry):
@@ -154,7 +165,8 @@
 
     top, wide = u_all.shape
     chunk = 256
-    half = spread.shape[0] // chunk // 2
+    pieces = spread.shape[0] // chunk
+    deep = ny * rows
     tile = 512
     dot = functools.partial(jnp.dot, preferred_element_type=F32)
     dot_t = functools.partial(lax.dot_general, dimension_numbers=(((0,), (0,)), ((), ())),
@@ -171,13 +183,14 @@
     def add_diag(part, product, span):
         diag_ref[:, span] += jnp.sum(part.astype(F32) * product, axis=0, keepdims=True)
 
-    def compute(zz, yy):
-        at = pl.ds(pl.multiple_of((zz * ny + yy) * rows, rows), rows)
+    def compute(zz):
+        at = pl.ds(pl.multiple_of(zz * deep, deep), deep)
         cross = (-dot(g_all[at, :], u_all[...])).astype(BF16)
 
-        @pl.when(jnp.logical_and(zz == z, yy == y))
-        def _():
-            cross_out[...] = cross
+        @pl.when(zz == z)
+        def _():
+            crossed[...] = cross
+            cross_out[...] = crossed[pl.ds(pl.multiple_of(y * rows, rows), rows), :]
         projected[...] += dot_t(u_all[at, :], cross)
 
         @pl.loop(0, y_ref.shape[1] // tile)
@@ -193,53 +206,74 @@
     low[...] = jnp.zeros_like(low)
     diag_ref[...] = bdiag_ref[...]
 
+    def cut(i):
+        return pieces * i // (nz + 2)
+
+    def g_group(k):
+        zz = nearest(z, k, nz)
+        over_y(lambda yy: g_event(zz, yy, x, True))
+
+    def x_group(k):
+        zz = nearest(z, k, nz)
+        over_y(lambda yy: over_x(1, lambda xx: g_event(zz, yy, xx, True)))
+
+    def b_group(k):
+        zz = nearest(z, k, nz)
+        over_y(lambda yy: b_event(zz, yy, True))
+
+    column(0, True, True)
+    g_event(z, y, x, True)
+    column(1, True)
+    u_event(z, y, True)
+    column(0, True, False)
+    column(2, True)
+    leaf_copy.wait()
+    place(0, cut(1))
+    over_y(lambda yy: g_event(z, yy, x, True), 1)
+    place(cut(1), cut(2))
+    g_group(1)
+    over_y(lambda yy: u_event(z, yy, True), 1)
+    place(cut(2), cut(3))
+
+    def u_group(k, carry):
+        zz = nearest(z, k, nz)
+        over_y(lambda yy: u_event(zz, yy, True))
+        place(cut(k + 2), cut(k + 3))
+        return carry
+    lax.fori_loop(1, nz, u_group, 0)
+    x_group(0)
+
     def group(k, carry):
         @pl.when(k < nz)
         def _():
-            zz = nearest(z, k, nz)
-            over_y(lambda yy: g_event(zz, yy, x, True))
-
-        @pl.when(k == 0)
-        def _():
-            over_y(lambda yy: u_event(nearest(z, 0, nz), yy, True))
-            leaf_copy.wait()
-            place(0, half)
-            over_y(lambda yy: u_event(nearest(z, 1, nz), yy, True))
-
-        @pl.when(k == 1)
-        def _():
-            over_y(lambda yy: u_event(nearest(z, 2, nz), yy, True))
-            place(half, 2 * half)
-
-            def rest(i, carry):
-                over_y(lambda yy: u_event(nearest(z, i, nz), yy, True))
+            g_group(k)
+
+        zz = nearest(z, k - 2, nz)
+
+        def rows_of(yy):
+            def peer(xx, carry):
+                index = (zz * ny + yy) * nx + xx
+                arrive(g_block(zz, yy, xx, 1 - core), g_send.at[index].at[4], g_peer.at[index])
                 return carry
-            lax.fori_loop(3, nz, rest, 0)
+            lax.fori_loop(0, nx, peer, 0)
+        over_y(rows_of)
+        compute(zz)
+
+        @pl.when(k == 2)
+        def _():
+            b_group(0)
+            b_group(1)
 
         @pl.when(k < nz)
         def _():
-            over_y(lambda yy: b_event(nearest(z, k, nz), yy, True))
-
-        @pl.when(k > 1)
-        def _():
-            zz = nearest(z, k - 2, nz)
-
-            def rows_of(yy):
-                def peer(xx, carry):
-                    index = (zz * ny + yy) * nx + xx
-                    arrive(g_block(zz, yy, xx, 1 - core), g_send.at[index].at[6], g_peer.at[index])
-                    return carry
-                lax.fori_loop(0, nx, peer, 0)
-                compute(zz, yy)
-            over_y(rows_of)
-
-        @pl.when(jnp.logical_and(k > 0, k <= nz))
-        def _():
-            zz = nearest(z, k - 1, nz)
-            over_y(lambda yy: over_x(1, lambda xx: g_event(zz, yy, xx, True)))
+            b_group(k)
+
+        @pl.when(k <= nz)
+        def _():
+            x_group(k - 1)
         return carry
 
-    lax.fori_loop(0, nz + 2, group, 0)
+    lax.fori_loop(2, nz + 2, group, 0)
 
     block[...] = (b_all[...] - projected[...]).astype(BF16)
     mid_out[...] = block[pl.ds(pl.multiple_of((z * ny + y) * mid, mid), mid), :]
@@ -251,6 +285,9 @@
         product = low[:, span] + dot(block[...], part)
         y_ref[top:, span] = (-product).astype(BF16)
         add_diag(part, product, span)
+
+    for which in range(3):
+        column(which, False)
 
     def finish(zz, carry):
         def inner(yy, carry):
@@ -291,8 +328,9 @@
             pltpu.VMEM((top, top), BF16), pltpu.VMEM((top, wide), BF16), pltpu.VMEM((wide, wide), F32),
             pltpu.VMEM((slots, columns), BF16), pltpu.VMEM((top + wide, columns), BF16),
             pltpu.VMEM((wide, columns), F32), pltpu.VMEM((wide, wide), F32), pltpu.VMEM((wide, wide), BF16),
-            dma((4,)), dma((n,)), dma((n,)), dma((n, 7)),
-            dma((n_sub,)), dma((n_sub, 7)), dma((n_sub,)), dma((n_sub, 7)),
+            pltpu.VMEM((top // nz, wide), BF16),
+            dma((4,)), dma((3, nz)), dma((n,)), dma((n,)), dma((n, 5)),
+            dma((n_sub,)), dma((n_sub, 5)), dma((n_sub,)), dma((n_sub, 5)),
         ],
         compiler_params=pltpu.CompilerParams(collective_id=0, has_side_effects=True,
                                              vmem_limit_bytes=60 * 2**20),

time: 150 us -> 160 us (1.067)
  Pallas kernels: 141 us -> 151 us
    pallas_call x1, Pallas kernels: 127 us -> 137 us  [gather_all(): pl.pallas_call(functools.partial(gather_kernel, nx, ny, nz), out_shape=(j...]
where the time goes in v3:
time: 160 us
  Pallas kernels  151 us (94%)
  local copies, waits for them, and re-layouts  5.45 us (3%)
  other arithmetic  2 us (1%)
    pallas_call x1, Pallas kernels, gather_all(): pl.pallas_call(functools.partial(gather_kernel, nx, ny, nz), out_shape=(j...  137 us
    pallas_call x1, Pallas kernels, pick_rows(): pl.pallas_call(pick_kernel, grid=(slots // tile,), out_shape=jax.ShapeDty...  14.3 us
    unnamed x11, local copies, waits for them, and re-layouts  5.16 us

profile of v3, /device:TPU:0, one launch (start us, length us, event | category | flops | bytes accessed | tf_op | source)
XLA Modules:
  0.0 160.0 jit_solution(14343360994572910548)
XLA Ops:
  1.3 0.7 fusion
  2.0 1.3 compare_select_fusion.across_ref
  3.3 0.3 copy.11.down_ref
  3.6 136.9 %shard_map.102 = (bf16[256,512]{1,0:T(8,128)(2,1)}, bf16[64,512]{1,0:T(8,128)(2,1)}, bf16[2560,1536]{1,0:T(8,128)(2,1)}, f32[1,1536]{1,0:T(1,128)}) custom-call(bf16[256,512]{1,0:T(8,128)(2,1)} %g_ref.1, bf16[256,512]{1,0:T(8,128)(2,1)} %bitcast.13, f32[64,512]{1,0:T(8,128)} %bitcast.15, s32[1,1536]{1,0:T(1,128)} %compare_select_fusion.across_ref, ...), custom_call_target="tpu_custom_call" | custom-call | tf_op jit(solution)/shard_map/pallas_call | solution.py:317
  140.5 0.0 copy-start
  140.5 3.2 %copy-done = bf16[2560,1536]{1,0:T(8,128)(2,1)S(1)} copy-done((bf16[2560,1536]{1,0:T(8,128)(2,1)S(1)}, bf16[2560,1536]{1,0:T(8,128)(2,1)}, u32[]{:S(2)}) %copy-start) | copy-done | bytes 7864344
  143.7 0.0 copy-start.1
  143.7 0.0 copy-start.2
  143.7 0.0 copy-start.3
  143.7 14.3 %shard_map.103 = bf16[1536,1536]{1,0:T(8,128)(2,1)} custom-call(s32[1536,1]{1,0:T(8,128)S(1)} %copy.11.down_ref, bf16[2560,1536]{1,0:T(8,128)(2,1)S(1)} %copy-done), custom_call_target="tpu_custom_call" | custom-call | tf_op jit(solution)/shard_map/pallas_call | solution.py:349
  158.1 0.0 copy-done.1
  158.1 0.7 copy.16
  158.8 0.0 copy-done.2
  158.8 0.6 copy.17
  159.4 0.0 copy-done.3
  159.4 0.6 copy.18
Async XLA Ops:
  140.5 3.2 %copy-start = (bf16[2560,1536]{1,0:T(8,128)(2,1)S(1)}, bf16[2560,1536]{1,0:T(8,128)(2,1)}, u32[]{:S(2)}) copy-start(bf16[2560,1536]{1,0:T(8,128)(2,1)} %get-tuple-element.10.y_ref) | copy-start | bytes 23592964
  143.7 14.4 %copy-start.1 = (bf16[256,512]{1,0:T(8,128)(2,1)S(1)}, bf16[256,512]{1,0:T(8,128)(2,1)}, u32[]{:S(2)}) copy-start(bf16[256,512]{1,0:T(8,128)(2,1)} %get-tuple-element.8) | copy-start | bytes 786436
  143.7 15.1 %copy-start.2 = (bf16[64,512]{1,0:T(8,128)(2,1)S(1)}, bf16[64,512]{1,0:T(8,128)(2,1)}, u32[]{:S(2)}) copy-start(bf16[64,512]{1,0:T(8,128)(2,1)} %get-tuple-element.9) | copy-start | bytes 196612
  143.7 15.7 %copy-start.3 = (f32[1,1536]{1,0:T(1,128)S(1)}, f32[1,1536]{1,0:T(1,128)}, u32[]{:S(2)}) copy-start(f32[1,1536]{1,0:T(1,128)} %get-tuple-element.19) | copy-start | bytes 18436

commit v4 on v2

--- a/solution.py
+++ b/solution.py
@@ -20,7 +20,7 @@
     return jnp.where(k <= 2 * room, near, far)
 
 
-def gather_kernel(nx, ny, nz, g_ref, u_ref, b_ref, across_ref, bdiag_ref, leaf_ref,
+def gather_kernel(nx, ny, nz, g_ref, u_ref, b_ref, across_ref, bdiag_ref, leaf_ref, exact_ref,
                   cross_out, mid_out, y_ref, diag_ref,
                   g_all, u_all, b_all, leaf_all, spread, low, projected, block,
                   own_sem, g_recv, g_peer, g_send, u_recv, u_send, b_recv, b_send):
@@ -154,7 +154,7 @@
 
     top, wide = u_all.shape
     chunk = 256
-    half = spread.shape[0] // chunk // 2
+    pieces = spread.shape[0] // chunk
     tile = 512
     dot = functools.partial(jnp.dot, preferred_element_type=F32)
     dot_t = functools.partial(lax.dot_general, dimension_numbers=(((0,), (0,)), ((), ())),
@@ -193,56 +193,50 @@
     low[...] = jnp.zeros_like(low)
     diag_ref[...] = bdiag_ref[...]
 
+    def x_group(k):
+        zz = nearest(z, k, nz)
+        over_y(lambda yy: over_x(1, lambda xx: g_event(zz, yy, xx, True)))
+
+    leaf_copy.wait()
+
+    def travel(k, carry):
+        zz = nearest(z, k, nz)
+        over_y(lambda yy: g_event(zz, yy, x, True))
+        over_y(lambda yy: u_event(zz, yy, True))
+        over_y(lambda yy: b_event(zz, yy, True))
+        place(pieces * k // nz, pieces * (k + 1) // nz)
+
+        @pl.when(k > 1)
+        def _():
+            x_group(k - 2)
+        return carry
+
+    lax.fori_loop(0, nz, travel, 0)
+
     def group(k, carry):
-        @pl.when(k < nz)
-        def _():
-            zz = nearest(z, k, nz)
-            over_y(lambda yy: g_event(zz, yy, x, True))
-
-        @pl.when(k == 0)
-        def _():
-            over_y(lambda yy: u_event(nearest(z, 0, nz), yy, True))
-            leaf_copy.wait()
-            place(0, half)
-            over_y(lambda yy: u_event(nearest(z, 1, nz), yy, True))
-
-        @pl.when(k == 1)
-        def _():
-            over_y(lambda yy: u_event(nearest(z, 2, nz), yy, True))
-            place(half, 2 * half)
-
-            def rest(i, carry):
-                over_y(lambda yy: u_event(nearest(z, i, nz), yy, True))
+        zz = nearest(z, k, nz)
+
+        def rows_of(yy):
+            def peer(xx, carry):
+                index = (zz * ny + yy) * nx + xx
+                arrive(g_block(zz, yy, xx, 1 - core), g_send.at[index].at[6], g_peer.at[index])
                 return carry
-            lax.fori_loop(3, nz, rest, 0)
-
-        @pl.when(k < nz)
-        def _():
-            over_y(lambda yy: b_event(nearest(z, k, nz), yy, True))
-
-        @pl.when(k > 1)
-        def _():
-            zz = nearest(z, k - 2, nz)
-
-            def rows_of(yy):
-                def peer(xx, carry):
-                    index = (zz * ny + yy) * nx + xx
-                    arrive(g_block(zz, yy, xx, 1 - core), g_send.at[index].at[6], g_peer.at[index])
-                    return carry
-                lax.fori_loop(0, nx, peer, 0)
-                compute(zz, yy)
-            over_y(rows_of)
-
-        @pl.when(jnp.logical_and(k > 0, k <= nz))
-        def _():
-            zz = nearest(z, k - 1, nz)
-            over_y(lambda yy: over_x(1, lambda xx: g_event(zz, yy, xx, True)))
+            lax.fori_loop(0, nx, peer, 0)
+            compute(zz, yy)
+        over_y(rows_of)
+
+        @pl.when(k < 2)
+        def _():
+            x_group(k + nz - 2)
         return carry
 
-    lax.fori_loop(0, nz + 2, group, 0)
-
-    block[...] = (b_all[...] - projected[...]).astype(BF16)
-    mid_out[...] = block[pl.ds(pl.multiple_of((z * ny + y) * mid, mid), mid), :]
+    lax.fori_loop(0, nz, group, 0)
+
+    block[...] = (b_all[...].astype(F32) - projected[...]).astype(BF16)
+    own_rows = pl.ds(pl.multiple_of((z * ny + y) * mid, mid), mid)
+    exact = (exact_ref[...] - projected[own_rows, :]).astype(BF16)
+    block[own_rows, :] = exact
+    mid_out[...] = exact
 
     @pl.loop(0, y_ref.shape[1] // tile)
     def _(j):
@@ -285,10 +279,10 @@
             jax.ShapeDtypeStruct((top + wide, columns), BF16),
             jax.ShapeDtypeStruct((1, columns), F32),
         ),
-        in_specs=[any_space] * 3 + [vmem] * 2 + [any_space],
+        in_specs=[any_space] * 3 + [vmem] * 2 + [any_space, vmem],
         out_specs=(vmem,) * 4,
         scratch_shapes=[
-            pltpu.VMEM((top, top), BF16), pltpu.VMEM((top, wide), BF16), pltpu.VMEM((wide, wide), F32),
+            pltpu.VMEM((top, top), BF16), pltpu.VMEM((top, wide), BF16), pltpu.VMEM((wide, wide), BF16),
             pltpu.VMEM((slots, columns), BF16), pltpu.VMEM((top + wide, columns), BF16),
             pltpu.VMEM((wide, columns), F32), pltpu.VMEM((wide, wide), F32), pltpu.VMEM((wide, wide), BF16),
             dma((4,)), dma((n,)), dma((n,)), dma((n, 7)),
@@ -296,7 +290,7 @@
         ],
         compiler_params=pltpu.CompilerParams(collective_id=0, has_side_effects=True,
                                              vmem_limit_bytes=60 * 2**20),
-    )(g_top, u_mid, b_mid, across, bdiag, u_leaf)
+    )(g_top, u_mid, b_mid.astype(BF16), across, bdiag, u_leaf, b_mid)
 
 
 def pick_kernel(down_ref, y_ref, off_ref):

time: 150 us -> 150 us (level)
  Pallas kernels: 141 us -> 139 us
  other arithmetic: 2 us -> 3.54 us
    pallas_call x1, Pallas kernels: 127 us -> 125 us  [gather_all(): pl.pallas_call(functools.partial(gather_kernel, nx, ny, nz), out_shape=(j...]
    convert_element_type x0 -> x1, other arithmetic: none -> 1.54 us  [gather_all(): b_mid.astype(BF16)]
where the time goes in v4:
time: 150 us; the launch traced here: 149 us
  Pallas kernels  139 us (93%)
  local copies, waits for them, and re-layouts  5.45 us (4%)
  other arithmetic  3.54 us (2%)
    pallas_call x1, Pallas kernels, gather_all(): pl.pallas_call(functools.partial(gather_kernel, nx, ny, nz), out_shape=(j...  125 us
    pallas_call x1, Pallas kernels, pick_rows(): pl.pallas_call(pick_kernel, grid=(slots // tile,), out_shape=jax.ShapeDty...  14.3 us
    unnamed x11, local copies, waits for them, and re-layouts  5.16 us

profile of v4, /device:TPU:0, one launch (start us, length us, event | category | flops | bytes accessed | tf_op | source)
XLA Modules:
  0.0 149.3 jit_solution(15561940508526813204)
XLA Ops:
  1.3 0.7 fusion
  2.0 1.3 compare_select_fusion.across_ref
  3.3 1.5 %bitcast_convert_fusion.b_ref = bf16[64,512]{1,0:T(8,128)(2,1)} fusion(f32[1,64,512]{2,1,0:T(8,128)} %param.9), kind=kLoop, calls=%fused_computation.1 | loop fusion | flops 32768 | bytes 196608 | tf_op jit(solution)/shard_map/convert_element_type | solution.py:293
  4.8 0.3 copy.11.down_ref
  5.1 124.6 %shard_map.102 = (bf16[256,512]{1,0:T(8,128)(2,1)}, bf16[64,512]{1,0:T(8,128)(2,1)}, bf16[2560,1536]{1,0:T(8,128)(2,1)}, f32[1,1536]{1,0:T(1,128)}) custom-call(bf16[256,512]{1,0:T(8,128)(2,1)} %g_ref.1, bf16[256,512]{1,0:T(8,128)(2,1)} %bitcast.15, bf16[64,512]{1,0:T(8,128)(2,1)} %bitcast_convert_fusion.b_ref, s32[1,1536]{1,0:T(1,128)} %compare_select_fusion.across_ref, ...), custom_call_target="tpu_custom_call" | custom-call | tf_op jit(solution)/shard_map/pallas_call | solution.py:274
  129.8 0.0 copy-start
  129.8 3.2 %copy-done = bf16[2560,1536]{1,0:T(8,128)(2,1)S(1)} copy-done((bf16[2560,1536]{1,0:T(8,128)(2,1)S(1)}, bf16[2560,1536]{1,0:T(8,128)(2,1)}, u32[]{:S(2)}) %copy-start) | copy-done | bytes 7864344
  133.0 0.0 copy-start.1
  133.0 0.0 copy-start.2
  133.0 0.0 copy-start.3
  133.0 14.3 %shard_map.103 = bf16[1536,1536]{1,0:T(8,128)(2,1)} custom-call(s32[1536,1]{1,0:T(8,128)S(1)} %copy.11.down_ref, bf16[2560,1536]{1,0:T(8,128)(2,1)S(1)} %copy-done), custom_call_target="tpu_custom_call" | custom-call | tf_op jit(solution)/shard_map/pallas_call | solution.py:305
  147.3 0.0 copy-done.1
  147.3 0.7 copy.16
  148.0 0.0 copy-done.2
  148.0 0.6 copy.17
  148.7 0.0 copy-done.3
  148.7 0.6 copy.18
Async XLA Ops:
  129.8 3.2 %copy-start = (bf16[2560,1536]{1,0:T(8,128)(2,1)S(1)}, bf16[2560,1536]{1,0:T(8,128)(2,1)}, u32[]{:S(2)}) copy-start(bf16[2560,1536]{1,0:T(8,128)(2,1)} %get-tuple-element.10.y_ref) | copy-start | bytes 23592964
  133.0 14.4 %copy-start.1 = (bf16[256,512]{1,0:T(8,128)(2,1)S(1)}, bf16[256,512]{1,0:T(8,128)(2,1)}, u32[]{:S(2)}) copy-start(bf16[256,512]{1,0:T(8,128)(2,1)} %get-tuple-element.8) | copy-start | bytes 786436
  133.0 15.1 %copy-start.2 = (bf16[64,512]{1,0:T(8,128)(2,1)S(1)}, bf16[64,512]{1,0:T(8,128)(2,1)}, u32[]{:S(2)}) copy-start(bf16[64,512]{1,0:T(8,128)(2,1)} %get-tuple-element.9) | copy-start | bytes 196612
  133.0 15.7 %copy-start.3 = (f32[1,1536]{1,0:T(1,128)S(1)}, f32[1,1536]{1,0:T(1,128)}, u32[]{:S(2)}) copy-start(f32[1,1536]{1,0:T(1,128)} %get-tuple-element.19) | copy-start | bytes 18436
